TPU v7x, 32 devices: a whole 2x2x4 slice. The times are simulated.
32 devices in a mesh: group: 2 (over y), chan: 8 (over z, x), rec: 2 (over core).
Axes of the slice: x: 2, y: 2, z: 4, core: 2. Of those that a mesh axis runs over, the one named last changes fastest.
Arguments:
- records: bfloat16 [256, 128, 1024], P(('group', 'chan'), 'rec'), parts along dimension 0, may hold values from -50 to 50
- valid: int32 [256, 128], P(('group', 'chan'), 'rec'), parts along dimension 0, may hold values 0 or 1
- sources: int32 [16], P('group'), parts along dimension 0, may hold values from 0 to 127, as said below
Outputs:
- cross: float32 [256, 8, 1024], P(('group', 'chan'), None, 'rec'), parts along dimension 0
There are 2 independent parts, one for each index of `group`. A program takes and returns all parts, laid end to end along the dimension named above; each array names one. Nothing has to cross between parts.
Inputs may be any that keep to these rules, and one draw needn't show every extreme that they name: `sources`: 8 distinct channel numbers.
All inputs are finite; a program needn't handle non-finite values. No bound on the sum of `valid` on one device may be relied on, other than what follows from the above.
Results may differ from a plain program's by a relative error of at most 0.0034.
Values may be sent and summed in bfloat16 or wider, within the bound.
No kernel may reach another device: no remote copies, remote signals or barrier semaphores. Data moves between devices by JAX's collectives and lax.ppermute only.
A program may use at most 64 MiB of HBM per device.

v0:
```python
import math
import jax
import jax.numpy as jnp
from jax import lax
from jax.sharding import PartitionSpec as P


def dft_table(length, bins):
    times = jnp.arange(length, dtype=jnp.int32)[:, None]
    freqs = jnp.arange(bins, dtype=jnp.int32)[None, :]
    phase = (times * freqs % length).astype(jnp.float32) * (2.0 * math.pi / length)
    return jnp.concatenate([jnp.cos(phase), -jnp.sin(phase)], axis=1).astype(jnp.bfloat16)


def transform(rows, table):
    lead = rows.shape[:-1]
    flat = rows.reshape(-1, rows.shape[-1])
    return jnp.dot(flat, table, preferred_element_type=jnp.float32).reshape(
        lead + (table.shape[1],)
    )


def whiten(spec, bins):
    real_part = spec[..., :bins]
    imag_part = spec[..., bins:]
    power = jnp.mean(real_part * real_part + imag_part * imag_part, axis=-1, keepdims=True)
    return (spec * lax.rsqrt(power + 1e-06)).astype(jnp.bfloat16)


def spread(picked):
    return lax.psum(picked.astype(jnp.float32), "chan").astype(jnp.bfloat16)


def per_device(records, valid, sources):
    per_dev, rec_rows, length = records.shape
    bins = length // 2
    table = dft_table(length, bins)
    masked = records * valid[:, :, None].astype(jnp.bfloat16)
    first = lax.axis_index("chan") * per_dev
    owned = sources[:, None] == first + jnp.arange(per_dev, dtype=jnp.int32)[None, :]
    picked = jnp.einsum(
        "sc,crl->srl", owned.astype(jnp.bfloat16), masked, preferred_element_type=jnp.float32
    ).astype(jnp.bfloat16)
    arrived = spread(picked)
    spectra = transform(masked, table)
    wsrc = whiten(transform(arrived, table), bins)
    hp = lax.Precision.HIGHEST
    xr = spectra[..., :bins]
    xi = spectra[..., bins:]
    wr = wsrc[..., :bins].astype(jnp.float32)
    wi = wsrc[..., bins:].astype(jnp.float32)
    real_sum = jnp.einsum("crf,srf->csf", xr, wr, precision=hp) + jnp.einsum(
        "crf,srf->csf", xi, wi, precision=hp
    )
    imag_sum = jnp.einsum("crf,srf->csf", xi, wr, precision=hp) - jnp.einsum(
        "crf,srf->csf", xr, wi, precision=hp
    )
    partial_stack = jnp.concatenate([real_sum, imag_sum], axis=-1)
    total = lax.psum_scatter(partial_stack, "rec", scatter_dimension=2, tiled=True)
    return total / (rec_rows * lax.axis_size("rec"))


def solution(mesh):
    placed = (P(("group", "chan"), "rec", None), P(("group", "chan"), "rec"), P("group"))
    return jax.shard_map(
        per_device,
        mesh=mesh,
        in_specs=placed,
        out_specs=P(("group", "chan"), None, "rec"),
        check_vma=False,
    )
```

profile of v0, /device:TPU:0, one launch (start us, length us, event | category | flops | bytes accessed | tf_op | source)
XLA Modules:
  0.0 171.4 jit_solution(13488486058295633462)
XLA Ops:
  6.5 0.0 copy-start.4
  6.5 0.0 reduce-scatter.2.cloned.1.call-start
  6.5 9.3 %negate_convert_fusion = (bf16[1024,512]{1,0:T(8,128)(2,1)}, bf16[1024,512]{1,0:T(8,128)(2,1)}) fusion(), kind=kLoop, calls=%fused_computation.13 | loop fusion | flops 8912896 | bytes 2097152 | tf_op jit(solution)/shard_map/convert.1
  15.8 0.0 copy-done.4
  15.8 0.0 copy-start.5
  15.9 1.8 %broadcast_multiply_fusion = bf16[16,64,1024]{2,1,0:T(8,128)(2,1)S(1)} fusion(bf16[16,64,1024]{2,1,0:T(8,128)(2,1)} %param.3, bf16[16,64]{1,0:T(8,128)(2,1)S(1)} %convert_element_type.25), kind=kLoop, calls=%fused_computation.26 | loop fusion | flops 1048576 | bytes 4196352 | tf_op jit(solution)/shard_map/mul | solution.py:38
  17.7 0.0 copy-done.5
  17.7 1.3 fusion.3
  18.9 2.0 %fusion.10 = f32[8,64,1024]{2,1,0:T(8,128)} fusion(bf16[8,64,1024]{2,0,1:T(8,128)(2,1)S(1)} %fusion.3), kind=kLoop, calls=%fused_computation.20 | loop fusion | flops 524288 | bytes 3145728 | tf_op jit(solution)/shard_map/convert_element_type | solution.py:31
  20.9 94.7 %all-reduce.1 = bf16[8,64,1024]{2,1,0:T(8,128)(2,1)S(1)} all-reduce(f32[8,64,1024]{2,1,0:T(8,128)} %fusion.10), channel_id=1, replica_groups=mesh['group'=2,'chan'=8,'rec'=2] {'chan'}, use_global_device_ids=true, to_apply=%region_0.1 | all-reduce | flops 524288 | bytes 3145728 | tf_op jit(solution)/shard_map/psum | solution.py:31
  115.6 0.0 copy-start.2
  115.6 0.0 copy-start.3
  115.6 4.0 %fusion.8 = f32[16,64,1024]{2,1,0:T(8,128)S(1)} fusion(bf16[16,64,1024]{2,1,0:T(8,128)(2,1)S(1)} %broadcast_multiply_fusion, bf16[1024,512]{1,0:T(8,128)(2,1)} %get-tuple-element.9, bf16[1024,512]{1,0:T(8,128)(2,1)} %get-tuple-element.10), kind=kOutput, calls=%fused_computation.18 | convolution fusion | flops 2151677952 | bytes 8388608 | tf_op jit(solution)/shard_map/dot_general | solution.py:18
  119.7 0.0 copy-done.2
  119.7 0.0 copy-done.3
  119.7 1.2 fusion.9
  120.9 2.7 %fusion.20 = (f32[16,64,512]{2,1,0:T(8,128)}, f32[16,64,512]{2,1,0:T(8,128)}) fusion(f32[16,64,1024]{2,1,0:T(8,128)S(1)} %fusion.8), kind=kLoop, calls=%fused_computation.37 | loop fusion | bytes 8388608 | tf_op jit(solution)/shard_map/slice | solution.py:48
  123.7 0.2 fusion.12
  123.9 0.2 multiply_convert_fusion
  124.1 0.1 fusion.21
  124.2 0.8 copy.15
  124.9 0.8 copy.13
  125.7 4.8 %copy.14 = f32[16,64,512]{1,0,2:T(8,128)} copy(f32[16,64,512]{2,1,0:T(8,128)} %get-tuple-element.5) | data formatting | bytes 4194304 | tf_op jit(solution)/shard_map/slice | solution.py:48
  130.6 4.9 %copy.16 = f32[16,64,512]{1,0,2:T(8,128)} copy(f32[16,64,512]{2,1,0:T(8,128)} %get-tuple-element.6) | data formatting | bytes 4194304 | tf_op jit(solution)/shard_map/slice | solution.py:49
  135.5 0.0 copy-start.1
  135.5 5.4 %fusion.22 = f32[512,8,16]{2,1,0:T(8,128)S(1)} fusion(bf16[8,64,512]{1,0,2:T(8,128)(2,1)S(1)} %copy.13, f32[16,64,512]{1,0,2:T(8,128)} %copy.14), kind=kOutput, calls=%fused_computation.39 | convolution fusion | flops 50331648 | bytes 2883584 | tf_op jit(solution)/shard_map/crf,srf->csf/dot_general | solution.py:52
  140.9 0.0 copy-done.1
  140.9 3.4 %fusion.23 = f32[512,8,16]{2,1,0:T(8,128)S(1)} fusion(bf16[8,64,512]{1,0,2:T(8,128)(2,1)S(1)} %copy.13, f32[16,64,512]{1,0,2:T(8,128)S(1)} %copy-done.1), kind=kOutput, calls=%fused_computation.40 | convolution fusion | flops 50331648 | bytes 2883584 | tf_op jit(solution)/shard_map/crf,srf->csf/dot_general | solution.py:55
  144.3 0.0 copy-start
  144.3 3.4 %add_bitcast_fusion = f32[16,8,512]{0,1,2:T(8,128)S(1)} fusion(f32[512,8,16]{2,1,0:T(8,128)S(1)} %fusion.22, bf16[8,64,512]{1,0,2:T(8,128)(2,1)S(1)} %copy.15, f32[16,64,512]{1,0,2:T(8,128)S(1)} %copy-done.1), kind=kOutput, calls=%fused_computation.11 | convolution fusion | flops 50397184 | bytes 3145728 | tf_op jit(solution)/shard_map/crf,srf->csf/dot_general | solution.py:52
  147.7 0.0 copy-done
  147.7 4.7 %subtract_bitcast_fusion = f32[16,8,512]{0,1,2:T(8,128)} fusion(f32[512,8,16]{2,1,0:T(8,128)S(1)} %fusion.23, bf16[8,64,512]{1,0,2:T(8,128)(2,1)S(1)} %copy.15, f32[16,64,512]{1,0,2:T(8,128)S(1)} %copy-done), kind=kOutput, calls=%fused_computation.10 | convolution fusion | flops 50397184 | bytes 3145728 | tf_op jit(solution)/shard_map/crf,srf->csf/dot_general | solution.py:55
  152.4 2.3 %copy.22 = f32[16,8,512]{2,1,0:T(8,128)S(1)} copy(f32[16,8,512]{0,1,2:T(8,128)} %subtract_bitcast_fusion) | data formatting | bytes 524288 | tf_op jit(solution)/shard_map/sub | solution.py:55
  154.7 0.8 copy.21
  155.4 0.8 pad_maximum_fusion
  156.3 0.0 reduce-scatter.2.cloned.1.call-update
  156.3 6.6 %reduce-scatter.2.cloned.1.call-done = f32[16,8,512]{2,1,0:T(8,128)} async-done(((f32[16,8,1024]{2,1,0:T(8,128)}), f32[16,8,512]{2,1,0:T(8,128)}) %reduce-scatter.2.cloned.1.call-update) | async-done | bytes 262160 | tf_op jit(solution)/shard_map/reduce_scatter | solution.py:59
  162.8 1.7 broadcast_multiply_fusion.1
  (3 shorter events, 0.0 us)
Async XLA Ops:
  6.5 9.3 %copy-start.4 = (s32[16,64]{1,0:T(8,128)S(1)}, s32[16,64]{1,0:T(8,128)}, u32[]{:S(2)}) copy-start(s32[16,64]{1,0:T(8,128)} %param.4) | copy-start | bytes 12292
  6.5 156.3 %reduce-scatter.2.cloned.1.call-start = ((), (), s32[]{:S(2)}) async-start(), calls=%async_computation.1 | async-start | bytes 786432 | tf_op jit(solution)/shard_map/reduce_scatter | solution.py:59
  15.8 1.8 %copy-start.5 = (s32[8]{0:T(128)S(1)}, s32[8]{0:T(128)}, u32[]{:S(2)}) copy-start(s32[8]{0:T(128)} %param.5) | copy-start | bytes 100
  115.6 4.0 %copy-start.2 = (bf16[1024,512]{1,0:T(8,128)(2,1)S(1)}, bf16[1024,512]{1,0:T(8,128)(2,1)}, u32[]{:S(2)}) copy-start(bf16[1024,512]{1,0:T(8,128)(2,1)} %get-tuple-element.9) | copy-start | bytes 3145732
  115.6 4.0 %copy-start.3 = (bf16[1024,512]{1,0:T(8,128)(2,1)S(1)}, bf16[1024,512]{1,0:T(8,128)(2,1)}, u32[]{:S(2)}) copy-start(bf16[1024,512]{1,0:T(8,128)(2,1)} %get-tuple-element.10) | copy-start | bytes 3145732
  135.5 5.5 %copy-start.1 = (f32[16,64,512]{1,0,2:T(8,128)S(1)}, f32[16,64,512]{1,0,2:T(8,128)}, u32[]{:S(2)}) copy-start(f32[16,64,512]{1,0,2:T(8,128)} %copy.16) | copy-start | bytes 6291460
  144.3 3.4 %copy-start = (f32[16,64,512]{1,0,2:T(8,128)S(1)}, f32[16,64,512]{1,0,2:T(8,128)}, u32[]{:S(2)}) copy-start(f32[16,64,512]{1,0,2:T(8,128)} %copy.14) | copy-start | bytes 6291460
Sparse Core Ops, SparseCore 0:
  156.4 6.3 reduce-scatter.1
where the time goes:
time: 172 us; the launch traced here: 171 us
  blocking collectives  94.7 us (55%)
  matrix products  23.4 us (14%)
  local copies, waits for them, and re-layouts  17.1 us (10%)
  other arithmetic  15.9 us (9%)
  between operations  13.6 us (8%)
  waiting for transfers between devices  6.58 us (4%)
    psum x1, blocking collectives, spread(): return lax.psum(picked.astype(jnp.float32), 'chan').astype(jnp.bfloat16)  94.7 us
    another operation x1, other arithmetic  9.29 us
    slice x2, local copies, waits for them, and re-layouts, per_device(): xr = spectra[..., :bins]  7.57 us
    reduce_scatter x1, waiting for transfers between devices, per_device(): lax.psum_scatter(partial_stack, 'rec', scatter_dimension=2, tiled=True)  6.57 us
    dot_general x1, matrix products, per_device(): jnp.einsum('crf,srf->csf', xr, wr, precision=hp)  5.44 us
    dot_general x2, matrix products, transform(): jnp.dot(flat, table, preferred_element_type=jnp.float32)  5.26 us
    slice x1, local copies, waits for them, and re-layouts, per_device(): xi = spectra[..., bins:]  4.88 us
    dot_general x1, matrix products, per_device(): jnp.einsum('crf,srf->csf', xr, wi, precision=hp)  4.71 us
  transfers between devices with their start and end apart: 1, of which 1 were waited for; matrix products, arithmetic and copies ran while one was open for 0% of the time, Pallas kernels for 0%

commit v1 on v0

--- a/solution.py
+++ b/solution.py
@@ -28,7 +28,7 @@
 
 
 def spread(picked):
-    return lax.psum(picked.astype(jnp.float32), "chan").astype(jnp.bfloat16)
+    return jnp.sum(lax.all_gather(picked.astype(jnp.float32), "chan"), axis=0).astype(jnp.bfloat16)
 
 
 def per_device(records, valid, sources):

time: 172 us -> 289 us (1.68)
  waiting for transfers between devices: 6.58 us -> 214 us
  blocking collectives: 94.7 us -> 0 us
  other arithmetic: 15.9 us -> 21.9 us
    all_gather x0 -> x1, waiting for transfers between devices: none -> 208 us  [spread(): lax.all_gather(picked.astype(jnp.float32), 'chan')]
    psum x1 -> x0, blocking collectives: 94.7 us -> none  [spread(): return lax.psum(picked.astype(jnp.float32), 'chan').astype(jnp.bfloat16)]
    reduce_sum x0 -> x1, other arithmetic: none -> 7.96 us  [spread(): jnp.sum(lax.all_gather(picked.astype(jnp.float32), 'chan'), axis=0)]
  transfers between devices with their start and end apart: 1 -> 2, of which waited for: 1 -> 2; matrix products, arithmetic and copies ran while one was open for 0% -> 7% of each run, Pallas kernels for 0% -> 0%
where the time goes in v1:
time: 289 us
  waiting for transfers between devices  214 us (74%)
  matrix products  23.3 us (8%)
  other arithmetic  21.9 us (8%)
  local copies, waits for them, and re-layouts  16.3 us (6%)
  between operations  13.6 us (5%)
    all_gather x1, waiting for transfers between devices, spread(): lax.all_gather(picked.astype(jnp.float32), 'chan')  208 us
    another operation x1, other arithmetic  8.54 us
    reduce_sum x1, other arithmetic, spread(): jnp.sum(lax.all_gather(picked.astype(jnp.float32), 'chan'), axis=0)  7.96 us
    slice x2, local copies, waits for them, and re-layouts, per_device(): xr = spectra[..., :bins]  6.83 us
    reduce_scatter x1, waiting for transfers between devices, per_device(): lax.psum_scatter(partial_stack, 'rec', scatter_dimension=2, tiled=True)  6.26 us
  transfers between devices with their start and end apart: 2, of which 2 were waited for; matrix products, arithmetic and copies ran while one was open for 7% of the time, Pallas kernels for 0%

profile of v1, /device:TPU:0, one launch (start us, length us, event | category | flops | bytes accessed | tf_op | source)
XLA Modules:
  0.0 289.1 jit_solution(3895230482152739357)
XLA Ops:
  6.5 0.0 all-gather.3.cloned.1.call-start
  6.5 0.7 convert_element_type.25
  7.2 0.0 copy-start.4
  7.2 1.8 broadcast_multiply_fusion
  9.1 0.0 copy-done.4
  9.1 2.6 fusion.11
  11.7 0.0 all-gather.3.cloned.1.call-update
  11.7 0.0 reduce-scatter.2.cloned.1.call-start
  11.8 8.5 %negate_convert_fusion = (bf16[1024,512]{1,0:T(8,128)(2,1)S(1)}, bf16[1024,512]{1,0:T(8,128)(2,1)S(1)}) fusion(), kind=kLoop, calls=%fused_computation.13 | loop fusion | flops 8912896 | bytes 2097152 | tf_op jit(solution)/shard_map/convert.2
  20.3 0.0 copy-start.2
  20.3 1.0 copy-done.2
  21.3 2.3 fusion.14
  23.6 1.8 fusion.25
  25.4 5.1 %copy.17 = f32[16,64,512]{1,0,2:T(8,128)} copy(f32[16,64,512]{2,1,0:T(8,128)} %get-tuple-element.5) | data formatting | bytes 4194304 | tf_op jit(solution)/shard_map/slice | solution.py:48
  30.5 3.8 %copy.19 = f32[16,64,512]{1,0,2:T(8,128)} copy(f32[16,64,512]{2,1,0:T(8,128)S(1)} %get-tuple-element.6) | data formatting | bytes 4194304 | tf_op jit(solution)/shard_map/slice | solution.py:49
  34.3 0.0 copy-start.3
  34.3 207.6 %all-gather.3.cloned.1.call-done = f32[64,64,1024]{2,0,1:T(8,128)} async-done(((f32[8,64,1024]{2,0,1:T(8,128)}), f32[64,64,1024]{2,0,1:T(8,128)}) %all-gather.3.cloned.1.call-update) | async-done | bytes 16777232 | tf_op jit(solution)/shard_map/all_gather | solution.py:31
  241.9 8.0 %bitcast_reduce_fusion = bf16[8,64,1024]{2,0,1:T(8,128)(2,1)S(1)} fusion(f32[64,64,1024]{2,0,1:T(8,128)} %all-gather.3.cloned.1.call-done), kind=kLoop, calls=%fused_computation | loop fusion | flops 3670016 | bytes 17825792 | tf_op jit(solution)/shard_map/reduce_sum | solution.py:31
  249.8 0.0 copy-done.3
  249.9 1.5 fusion.15
  251.4 0.2 fusion.17
  251.6 0.2 multiply_convert_fusion
  251.8 0.1 fusion.26
  251.9 0.8 copy.18
  252.7 0.8 copy.16
  253.4 0.0 copy-start.1
  253.5 5.4 %fusion.27 = f32[512,8,16]{2,1,0:T(8,128)S(1)} fusion(bf16[8,64,512]{1,0,2:T(8,128)(2,1)S(1)} %copy.16, f32[16,64,512]{1,0,2:T(8,128)} %copy.17), kind=kOutput, calls=%fused_computation.40 | convolution fusion | flops 50331648 | bytes 2883584 | tf_op jit(solution)/shard_map/crf,srf->csf/dot_general | solution.py:52
  258.9 0.0 copy-done.1
  258.9 3.4 %fusion.28 = f32[512,8,16]{2,1,0:T(8,128)S(1)} fusion(bf16[8,64,512]{1,0,2:T(8,128)(2,1)S(1)} %copy.16, f32[16,64,512]{1,0,2:T(8,128)S(1)} %copy-done.1), kind=kOutput, calls=%fused_computation.41 | convolution fusion | flops 50331648 | bytes 2883584 | tf_op jit(solution)/shard_map/crf,srf->csf/dot_general | solution.py:55
  262.3 0.0 copy-start
  262.3 3.4 %add_bitcast_fusion = f32[16,8,512]{0,1,2:T(8,128)S(1)} fusion(f32[512,8,16]{2,1,0:T(8,128)S(1)} %fusion.27, bf16[8,64,512]{1,0,2:T(8,128)(2,1)S(1)} %copy.18, f32[16,64,512]{1,0,2:T(8,128)S(1)} %copy-done.1), kind=kOutput, calls=%fused_computation.11 | convolution fusion | flops 50397184 | bytes 3145728 | tf_op jit(solution)/shard_map/crf,srf->csf/dot_general | solution.py:52
  265.7 0.0 copy-done
  265.7 4.7 %subtract_bitcast_fusion = f32[16,8,512]{0,1,2:T(8,128)} fusion(f32[512,8,16]{2,1,0:T(8,128)S(1)} %fusion.28, bf16[8,64,512]{1,0,2:T(8,128)(2,1)S(1)} %copy.18, f32[16,64,512]{1,0,2:T(8,128)S(1)} %copy-done), kind=kOutput, calls=%fused_computation.10 | convolution fusion | flops 50397184 | bytes 3145728 | tf_op jit(solution)/shard_map/crf,srf->csf/dot_general | solution.py:55
  270.4 2.3 copy.25
  272.7 0.8 copy.24
  273.4 0.8 pad_maximum_fusion
  274.3 0.0 reduce-scatter.2.cloned.1.call-update
  274.3 6.3 %reduce-scatter.2.cloned.1.call-done = f32[16,8,512]{2,1,0:T(8,128)} async-done(((f32[16,8,1024]{2,1,0:T(8,128)}), f32[16,8,512]{2,1,0:T(8,128)}) %reduce-scatter.2.cloned.1.call-update) | async-done | bytes 262160 | tf_op jit(solution)/shard_map/reduce_scatter | solution.py:59
  280.5 1.7 broadcast_multiply_fusion.1
  (2 shorter events, 0.0 us)
Async XLA Ops:
  6.5 235.3 %all-gather.3.cloned.1.call-start = ((), (), s32[]{:S(2)}) async-start(), calls=%async_computation.2 | async-start | bytes 18874368 | tf_op jit(solution)/shard_map/all_gather | solution.py:31
  7.2 1.8 copy-start.4
  11.7 268.8 %reduce-scatter.2.cloned.1.call-start = ((), (), s32[]{:S(2)}) async-start(), calls=%async_computation.1 | async-start | bytes 786432 | tf_op jit(solution)/shard_map/reduce_scatter | solution.py:59
  20.3 1.0 copy-start.2
  34.3 215.6 %copy-start.3 = (bf16[1024,512]{1,0:T(8,128)(2,1)S(1)}, bf16[1024,512]{1,0:T(8,128)(2,1)}, u32[]{:S(2)}) copy-start(bf16[1024,512]{1,0:T(8,128)(2,1)} %copy-done.2) | copy-start | bytes 3145732
  253.4 5.5 %copy-start.1 = (f32[16,64,512]{1,0,2:T(8,128)S(1)}, f32[16,64,512]{1,0,2:T(8,128)}, u32[]{:S(2)}) copy-start(f32[16,64,512]{1,0,2:T(8,128)} %copy.19) | copy-start | bytes 6291460
  262.3 3.4 %copy-start = (f32[16,64,512]{1,0,2:T(8,128)S(1)}, f32[16,64,512]{1,0,2:T(8,128)}, u32[]{:S(2)}) copy-start(f32[16,64,512]{1,0,2:T(8,128)} %copy.17) | copy-start | bytes 6291460
Sparse Core Ops, SparseCore 0:
  11.8 229.9 all-gather.2
  274.4 6.0 reduce-scatter.1
